TPU v7x, 256 devices: a whole 4x4x8 slice. The times are simulated.
256 devices in a mesh: sec: 64 (over x, y_lo, z), tile: 4 (over y_hi, core).
Axes of the slice: x: 4, y: 4 (y_hi: 2, y_lo: 2; y = y_hi * 2 + y_lo), z: 8, core: 2. Of those that a mesh axis runs over, the one named last changes fastest.
Arguments:
- features: bfloat16 [64, 2048, 256], P('sec', 'tile'), may hold values from -16 to 16
- select: int32 [64, 2048], P('sec', 'tile'), may hold values from 1 to 7
- validity: int32 [64], P('sec'), may hold values 0 or 1
- offset_gain: float32 [3, 256], replicated, may hold values from 0.5 to 2
Outputs:
- aligned: bfloat16 [64, 2048, 256], P('sec', 'tile')
Inputs may be any that keep to these rules, and one draw needn't show every extreme that they name: `select`: bit k - 1 of a value is 1 where offset k votes.
All inputs are finite; a program needn't handle non-finite values. No bound on the sum of `validity` on one device may be relied on, other than what follows from the above.
Results may differ from a plain program's by a relative error of at most 0.0027.
Values may be sent and summed in bfloat16 or wider, within the bound.
A program may use at most 64 MiB of HBM per device.

v0:
```python
import math

import jax
import jax.numpy as jnp
from jax import lax
from jax.sharding import PartitionSpec as P

score_factor = 2.5


def laid_out(blocks, dim):
    blocks = jnp.moveaxis(blocks, 0, dim)
    shape = blocks.shape
    return blocks.reshape(*shape[:dim], shape[dim] * shape[dim + 1], *shape[dim + 2 :])


def copy_for_each(shard, axis):
    devices = lax.axis_size(axis)
    return lax.all_to_all(
        jnp.broadcast_to(shard[None], (devices, *shard.shape)), axis, 0, 0, tiled=True
    )


def collect(shard, axis, dim):
    return laid_out(copy_for_each(shard, axis), dim)


def from_behind(block, axis, distance):
    devices = range(lax.axis_size(axis))
    route = [(i - distance, i) for i in devices if i - distance in devices]
    return lax.ppermute(block, axis, route)


def make_step(queries, score_scale):

    def fold_step(state_tuple, key_piece, first_row):
        running_max, running_sum, weighted = state_tuple
        key_rows = key_piece[0]
        scores = jnp.dot(queries, key_rows.T, preferred_element_type=jnp.float32) * score_scale
        new_max = jnp.maximum(running_max, jnp.max(scores, axis=1))
        weights = jnp.exp(scores - new_max[:, None])
        running_sum = jnp.sum(weights, axis=1)
        weighted = jnp.dot(
            weights.astype(jnp.bfloat16), key_rows, preferred_element_type=jnp.float32
        )
        return (new_max, running_sum, weighted)

    return fold_step


def shards(features, select, validity, offset_gain):
    queries = features[0]
    num_rows, channels = queries.shape
    fold_step = make_step(queries, score_factor / math.sqrt(channels))
    initial = (
        jnp.full((num_rows,), -1e30, jnp.float32),
        jnp.zeros((num_rows,), jnp.float32),
        jnp.zeros((num_rows, channels), jnp.float32),
    )
    valid_flag = validity.astype(jnp.bfloat16)
    outcomes = []
    received, received_flag = (features, valid_flag)
    for offset in range(1, 4):
        received, received_flag = from_behind((received, received_flag), "sec", 1)
        final_max, final_sum, weighted = fold_step(
            initial, collect(received, "tile", 1), jnp.int32(0)
        )
        outcomes.append((weighted / final_sum[:, None], received_flag))
    numerator = jnp.zeros((num_rows, channels), jnp.float32)
    vote_count = jnp.zeros((num_rows,), jnp.float32)
    for offset_index in range(3):
        warped, received_flag = outcomes[offset_index]
        chosen = (select[0] // 2**offset_index % 2).astype(jnp.float32) * received_flag.astype(
            jnp.float32
        )[0]
        numerator = numerator + chosen[:, None] * offset_gain[offset_index][None, :] * warped
        vote_count = vote_count + chosen
    aligned = numerator / jnp.maximum(vote_count, 1.0)[:, None]
    return aligned.astype(jnp.bfloat16)[None]


def solution(mesh):
    in_specs = (P("sec", "tile", None), P("sec", "tile"), P("sec"), P())
    out_specs = P("sec", "tile", None)
    return jax.shard_map(shards, mesh=mesh, in_specs=in_specs, out_specs=out_specs, check_vma=False)
```

profile of v0, /device:TPU:7, one launch (start us, length us, event | category | flops | bytes accessed | tf_op | source)
XLA Modules:
  0.0 99.4 jit_solution(9521876216375194056)
XLA Ops:
  0.0 3.7 %collective-permute-start.1 = (bf16[1,512,256]{2,1,0:T(8,128)(2,1)}, bf16[1,512,256]{2,1,0:T(8,128)(2,1)S(1)}, u32[]{:S(2)}, u32[]{:S(2)}) collective-permute-start(bf16[1,512,256]{2,1,0:T(8,128)(2,1)} %param.4), channel_id=1, source_target_pairs={{0,4},{4,8},{8,12},{12,16},{16,20},{20,24},{24,28},{28,32},{32,36}... | collective-permute-start | bytes 786440 | tf_op jit(solution)/shard_map/ppermute | solution.py:31
  3.7 11.4 %collective-permute-done.1 = bf16[1,512,256]{2,1,0:T(8,128)(2,1)S(1)} collective-permute-done((bf16[1,512,256]{2,1,0:T(8,128)(2,1)}, bf16[1,512,256]{2,1,0:T(8,128)(2,1)S(1)}, u32[]{:S(2)}, u32[]{:S(2)}) %collective-permute-start.1) | collective-permute-done | bytes 262176 | tf_op jit(solution)/shard_map/ppermute | solution.py:31
  15.1 1.0 %broadcast_in_dim.17 = bf16[4,1,512,256]{3,2,1,0:T(8,128)(2,1)} broadcast(bf16[512,256]{1,0:T(8,128)(2,1)S(1)} %bitcast.44), dimensions={2,3} | broadcast | bytes 1310720 | tf_op jit(solution)/shard_map/broadcast_in_dim | solution.py:20
  16.1 5.4 %all-to-all-start = ((bf16[4,1,512,256]{3,2,1,0:T(8,128)(2,1)}), bf16[4,1,512,256]{3,2,1,0:T(8,128)(2,1)S(1)}, u32[]{:S(2)}, u32[]{:S(2)}) async-start(bf16[4,1,512,256]{3,2,1,0:T(8,128)(2,1)} %broadcast_in_dim.17), calls=%async_computation | async-start | bytes 2097152 | tf_op jit(solution)/shard_map/all_to_all | solution.py:19
  22.2 2.6 %collective-permute-start = (bf16[1]{0:T(256)(128)(2,1)}, bf16[1]{0:T(256)(128)(2,1)}, u32[]{:S(2)}, u32[]{:S(2)}) collective-permute-start(bf16[1]{0:T(256)(128)(2,1)} %convert_element_type.49), channel_id=1, source_target_pairs={{0,4},{4,8},{8,12},{12,16},{16,20},{20,24},{24,28},{28,32},{32,36}... | collective-permute-start | bytes 14 | tf_op jit(solution)/shard_map/ppermute | solution.py:31
  24.8 1.9 %collective-permute-start.3 = (bf16[1,512,256]{2,1,0:T(8,128)(2,1)S(1)}, bf16[1,512,256]{2,1,0:T(8,128)(2,1)S(1)}, u32[]{:S(2)}, u32[]{:S(2)}) collective-permute-start(bf16[1,512,256]{2,1,0:T(8,128)(2,1)S(1)} %collective-permute-done.1), channel_id=1, source_target_pairs={{0,4},{4,8},{8,12},{12,16},{16,20},{20,24},{24,28},{28,32},{32,36}... | collective-permute-start | bytes 786440 | tf_op jit(solution)/shard_map/ppermute | solution.py:31
  27.6 2.1 %collective-permute-done = bf16[1]{0:T(256)(128)(2,1)} collective-permute-done((bf16[1]{0:T(256)(128)(2,1)}, bf16[1]{0:T(256)(128)(2,1)}, u32[]{:S(2)}, u32[]{:S(2)}) %collective-permute-start) | collective-permute-done | bytes 34 | tf_op jit(solution)/shard_map/ppermute | solution.py:31
  30.3 1.9 %collective-permute-start.2 = (bf16[1]{0:T(256)(128)(2,1)}, bf16[1]{0:T(256)(128)(2,1)}, u32[]{:S(2)}, u32[]{:S(2)}) collective-permute-start(bf16[1]{0:T(256)(128)(2,1)} %collective-permute-done), channel_id=1, source_target_pairs={{0,4},{4,8},{8,12},{12,16},{16,20},{20,24},{24,28},{28,32},{32,36}... | collective-permute-start | bytes 14 | tf_op jit(solution)/shard_map/ppermute | solution.py:31
  32.3 5.8 %collective-permute-done.2 = bf16[1]{0:T(256)(128)(2,1)} collective-permute-done((bf16[1]{0:T(256)(128)(2,1)}, bf16[1]{0:T(256)(128)(2,1)}, u32[]{:S(2)}, u32[]{:S(2)}) %collective-permute-start.2) | collective-permute-done | bytes 34 | tf_op jit(solution)/shard_map/ppermute | solution.py:31
  38.6 1.9 %collective-permute-start.4 = (bf16[1]{0:T(256)(128)(2,1)}, bf16[1]{0:T(256)(128)(2,1)}, u32[]{:S(2)}, u32[]{:S(2)}) collective-permute-start(bf16[1]{0:T(256)(128)(2,1)} %collective-permute-done.2), channel_id=1, source_target_pairs={{0,4},{4,8},{8,12},{12,16},{16,20},{20,24},{24,28},{28,32},{32,36}... | collective-permute-start | bytes 14 | tf_op jit(solution)/shard_map/ppermute | solution.py:31
  40.6 5.6 %collective-permute-done.4 = bf16[1]{0:T(256)(128)(2,1)} collective-permute-done((bf16[1]{0:T(256)(128)(2,1)}, bf16[1]{0:T(256)(128)(2,1)}, u32[]{:S(2)}, u32[]{:S(2)}) %collective-permute-start.4) | collective-permute-done | bytes 34 | tf_op jit(solution)/shard_map/ppermute | solution.py:31
  47.5 1.9 %collective-permute-start.5 = (bf16[1,512,256]{2,1,0:T(8,128)(2,1)S(1)}, bf16[1,512,256]{2,1,0:T(8,128)(2,1)S(1)}, u32[]{:S(2)}, u32[]{:S(2)}) collective-permute-start(bf16[1,512,256]{2,1,0:T(8,128)(2,1)S(1)} %collective-permute-done.3), channel_id=1, source_target_pairs={{0,4},{4,8},{8,12},{12,16},{16,20},{20,24},{24,28},{28,32},{32,36}... | collective-permute-start | bytes 786440 | tf_op jit(solution)/shard_map/ppermute | solution.py:31
  49.5 1.0 %broadcast_in_dim.20 = bf16[4,1,512,256]{3,2,1,0:T(8,128)(2,1)} broadcast(bf16[512,256]{1,0:T(8,128)(2,1)S(1)} %bitcast.43), dimensions={2,3} | broadcast | bytes 1310720 | tf_op jit(solution)/shard_map/broadcast_in_dim | solution.py:20
  50.5 7.9 %all-to-all-start.1 = ((bf16[4,1,512,256]{3,2,1,0:T(8,128)(2,1)}), bf16[4,1,512,256]{3,2,1,0:T(8,128)(2,1)S(1)}, u32[]{:S(2)}, u32[]{:S(2)}) async-start(bf16[4,1,512,256]{3,2,1,0:T(8,128)(2,1)} %broadcast_in_dim.20), calls=%async_computation.1 | async-start | bytes 2097152 | tf_op jit(solution)/shard_map/all_to_all | solution.py:19
  59.2 1.9 %copy-done = f32[512,2048]{1,0:T(8,128)} copy-done((f32[512,2048]{1,0:T(8,128)}, f32[512,2048]{1,0:T(8,128)S(1)}, u32[]{:S(2)}) %copy-start) | copy-done | bytes 4194328
  62.0 11.4 %all-to-all-done.1 = bf16[4,1,512,256]{3,2,1,0:T(8,128)(2,1)S(1)} async-done(((bf16[4,1,512,256]{3,2,1,0:T(8,128)(2,1)}), bf16[4,1,512,256]{3,2,1,0:T(8,128)(2,1)S(1)}, u32[]{:S(2)}, u32[]{:S(2)}) %all-to-all-start.1) | async-done | bytes 1048608 | tf_op jit(solution)/shard_map/all_to_all | solution.py:19
  73.3 1.0 %broadcast_in_dim.22 = bf16[4,1,512,256]{3,2,1,0:T(8,128)(2,1)} broadcast(bf16[512,256]{1,0:T(8,128)(2,1)S(1)} %bitcast.45), dimensions={2,3} | broadcast | bytes 1310720 | tf_op jit(solution)/shard_map/broadcast_in_dim | solution.py:20
  74.4 4.5 %all-to-all-start.2 = ((bf16[4,1,512,256]{3,2,1,0:T(8,128)(2,1)}), bf16[4,1,512,256]{3,2,1,0:T(8,128)(2,1)S(1)}, u32[]{:S(2)}, u32[]{:S(2)}) async-start(bf16[4,1,512,256]{3,2,1,0:T(8,128)(2,1)} %broadcast_in_dim.22), calls=%async_computation.2 | async-start | bytes 2097152 | tf_op jit(solution)/shard_map/all_to_all | solution.py:19
  80.5 1.7 %fusion.33 = f32[512,256]{1,0:T(8,128)} fusion(bf16[2048,256]{1,0:T(8,128)(2,1)S(1)} %bitcast.40, f32[512,2048]{1,0:T(8,128)S(1)} %get-tuple-element.15, f32[512]{0:T(512)S(1)} %broadcast_maximum_fusion.1, f32[512]{0:T(512)S(1)} %fusion.2, f32[256]{0:T(256)S(1)} %bitcast.49, f32[512]{0:T(512)S(1)} %get-tuple-element.7), kind=kOutput, calls=%fused_computation.26 | convolution fusion | flops 540409856 | bytes 5774336 | tf_op jit(solution)/shard_map/dot_general | solution.py:43
  82.2 11.6 %all-to-all-done.2 = bf16[4,1,512,256]{3,2,1,0:T(8,128)(2,1)S(1)} async-done(((bf16[4,1,512,256]{3,2,1,0:T(8,128)(2,1)}), bf16[4,1,512,256]{3,2,1,0:T(8,128)(2,1)S(1)}, u32[]{:S(2)}, u32[]{:S(2)}) %all-to-all-start.2) | async-done | bytes 1048608 | tf_op jit(solution)/shard_map/all_to_all | solution.py:19
  93.8 0.8 multiply_reduce_fusion
  95.5 0.9 fusion.39
  96.4 1.3 %copy-done.1 = f32[512,2048]{1,0:T(8,128)S(1)} copy-done((f32[512,2048]{1,0:T(8,128)S(1)}, f32[512,2048]{1,0:T(8,128)}, u32[]{:S(2)}) %copy-start.1) | copy-done | bytes 4194328
  97.8 1.7 %fusion.48 = bf16[1,512,256]{2,1,0:T(8,128)(2,1)} fusion(f32[512,256]{1,0:T(8,128)S(1)} %fusion.39, f32[512,256]{1,0:T(8,128)S(1)} %copy-done.3, bf16[2048,256]{1,0:T(8,128)(2,1)S(1)} %bitcast.38, f32[512,2048]{1,0:T(8,128)S(1)} %copy-done.1, f32[512]{0:T(512)S(1)} %broadcast_maximum_fusion.2, f32[512]{0:T(512)S(1)} %get-tuple-element.5, f32[512]{0:T(512)S(1)} %fusion, ...), kind=kOutput, calls=%fused_computation.31 | convolution fusion | flops 540934144 | bytes 6562816 | tf_op jit(solution)/shard_map/dot_general | solution.py:43
  (19 shorter events, 5.8 us)
Async XLA Ops:
  0.0 58.4 %copy-start.2 = (bf16[1,512,256]{2,1,0:T(8,128)(2,1)S(1)}, bf16[1,512,256]{2,1,0:T(8,128)(2,1)}, u32[]{:S(2)}) copy-start(bf16[1,512,256]{2,1,0:T(8,128)(2,1)} %param.4) | copy-start | bytes 786436
  0.0 15.1 %collective-permute-start.1 = (bf16[1,512,256]{2,1,0:T(8,128)(2,1)}, bf16[1,512,256]{2,1,0:T(8,128)(2,1)S(1)}, u32[]{:S(2)}, u32[]{:S(2)}) collective-permute-start(bf16[1,512,256]{2,1,0:T(8,128)(2,1)} %param.4), channel_id=1, source_target_pairs={{0,4},{4,8},{8,12},{12,16},{16,20},{20,24},{24,28},{28,32},{32,36}... | collective-permute-start | bytes 786440 | tf_op jit(solution)/shard_map/ppermute | solution.py:31
  16.1 33.3 %all-to-all-start = ((bf16[4,1,512,256]{3,2,1,0:T(8,128)(2,1)}), bf16[4,1,512,256]{3,2,1,0:T(8,128)(2,1)S(1)}, u32[]{:S(2)}, u32[]{:S(2)}) async-start(bf16[4,1,512,256]{3,2,1,0:T(8,128)(2,1)} %broadcast_in_dim.17), calls=%async_computation | async-start | bytes 2097152 | tf_op jit(solution)/shard_map/all_to_all | solution.py:19
  22.2 7.4 %collective-permute-start = (bf16[1]{0:T(256)(128)(2,1)}, bf16[1]{0:T(256)(128)(2,1)}, u32[]{:S(2)}, u32[]{:S(2)}) collective-permute-start(bf16[1]{0:T(256)(128)(2,1)} %convert_element_type.49), channel_id=1, source_target_pairs={{0,4},{4,8},{8,12},{12,16},{16,20},{20,24},{24,28},{28,32},{32,36}... | collective-permute-start | bytes 14 | tf_op jit(solution)/shard_map/ppermute | solution.py:31
  24.8 22.7 %collective-permute-start.3 = (bf16[1,512,256]{2,1,0:T(8,128)(2,1)S(1)}, bf16[1,512,256]{2,1,0:T(8,128)(2,1)S(1)}, u32[]{:S(2)}, u32[]{:S(2)}) collective-permute-start(bf16[1,512,256]{2,1,0:T(8,128)(2,1)S(1)} %collective-permute-done.1), channel_id=1, source_target_pairs={{0,4},{4,8},{8,12},{12,16},{16,20},{20,24},{24,28},{28,32},{32,36}... | collective-permute-start | bytes 786440 | tf_op jit(solution)/shard_map/ppermute | solution.py:31
  30.3 7.7 %collective-permute-start.2 = (bf16[1]{0:T(256)(128)(2,1)}, bf16[1]{0:T(256)(128)(2,1)}, u32[]{:S(2)}, u32[]{:S(2)}) collective-permute-start(bf16[1]{0:T(256)(128)(2,1)} %collective-permute-done), channel_id=1, source_target_pairs={{0,4},{4,8},{8,12},{12,16},{16,20},{20,24},{24,28},{28,32},{32,36}... | collective-permute-start | bytes 14 | tf_op jit(solution)/shard_map/ppermute | solution.py:31
  38.6 7.5 %collective-permute-start.4 = (bf16[1]{0:T(256)(128)(2,1)}, bf16[1]{0:T(256)(128)(2,1)}, u32[]{:S(2)}, u32[]{:S(2)}) collective-permute-start(bf16[1]{0:T(256)(128)(2,1)} %collective-permute-done.2), channel_id=1, source_target_pairs={{0,4},{4,8},{8,12},{12,16},{16,20},{20,24},{24,28},{28,32},{32,36}... | collective-permute-start | bytes 14 | tf_op jit(solution)/shard_map/ppermute | solution.py:31
  47.5 14.4 %collective-permute-start.5 = (bf16[1,512,256]{2,1,0:T(8,128)(2,1)S(1)}, bf16[1,512,256]{2,1,0:T(8,128)(2,1)S(1)}, u32[]{:S(2)}, u32[]{:S(2)}) collective-permute-start(bf16[1,512,256]{2,1,0:T(8,128)(2,1)S(1)} %collective-permute-done.3), channel_id=1, source_target_pairs={{0,4},{4,8},{8,12},{12,16},{16,20},{20,24},{24,28},{28,32},{32,36}... | collective-permute-start | bytes 786440 | tf_op jit(solution)/shard_map/ppermute | solution.py:31
  50.5 22.8 %all-to-all-start.1 = ((bf16[4,1,512,256]{3,2,1,0:T(8,128)(2,1)}), bf16[4,1,512,256]{3,2,1,0:T(8,128)(2,1)S(1)}, u32[]{:S(2)}, u32[]{:S(2)}) async-start(bf16[4,1,512,256]{3,2,1,0:T(8,128)(2,1)} %broadcast_in_dim.20), calls=%async_computation.1 | async-start | bytes 2097152 | tf_op jit(solution)/shard_map/all_to_all | solution.py:19
  59.2 1.9 %copy-start = (f32[512,2048]{1,0:T(8,128)}, f32[512,2048]{1,0:T(8,128)S(1)}, u32[]{:S(2)}) copy-start(f32[512,2048]{1,0:T(8,128)S(1)} %get-tuple-element.17) | copy-start | bytes 12582916
  74.4 19.4 %all-to-all-start.2 = ((bf16[4,1,512,256]{3,2,1,0:T(8,128)(2,1)}), bf16[4,1,512,256]{3,2,1,0:T(8,128)(2,1)S(1)}, u32[]{:S(2)}, u32[]{:S(2)}) async-start(bf16[4,1,512,256]{3,2,1,0:T(8,128)(2,1)} %broadcast_in_dim.22), calls=%async_computation.2 | async-start | bytes 2097152 | tf_op jit(solution)/shard_map/all_to_all | solution.py:19
  95.5 2.2 %copy-start.1 = (f32[512,2048]{1,0:T(8,128)S(1)}, f32[512,2048]{1,0:T(8,128)}, u32[]{:S(2)}) copy-start(f32[512,2048]{1,0:T(8,128)} %copy-done) | copy-start | bytes 12582916
  95.5 2.3 %copy-start.3 = (f32[512,256]{1,0:T(8,128)S(1)}, f32[512,256]{1,0:T(8,128)}, u32[]{:S(2)}) copy-start(f32[512,256]{1,0:T(8,128)} %fusion.33) | copy-start | bytes 1572868
where the time goes:
time: 100 us; the launch traced here: 99.4 us
  waiting for transfers between devices  47.9 us (48%)
  starting transfers between devices  31.7 us (32%)
  local copies, waits for them, and re-layouts  7.26 us (7%)
  matrix products  6.7 us (7%)
  other arithmetic  3.19 us (3%)
  between operations  2.72 us (3%)
    ppermute x6, waiting for transfers between devices, from_behind(): return lax.ppermute(block, axis, route)  24.9 us
    all_to_all x3, waiting for transfers between devices, copy_for_each(): lax.all_to_all(jnp.broadcast_to(shard[None], (devices, *shard.shape)), ax...  23 us
    all_to_all x3, starting transfers between devices, copy_for_each(): lax.all_to_all(jnp.broadcast_to(shard[None], (devices, *shard.shape)), ax...  17.7 us
    ppermute x6, starting transfers between devices, from_behind(): return lax.ppermute(block, axis, route)  14 us
    dot_general x3, matrix products, fold_step(): jnp.dot(weights.astype(jnp.bfloat16), key_rows, preferred_element_type=jn...  4.22 us
    unnamed x8, local copies, waits for them, and re-layouts  3.34 us
    broadcast_in_dim x3, local copies, waits for them, and re-layouts, copy_for_each(): jnp.broadcast_to(shard[None], (devices, *shard.shape))  3.12 us
    dot_general x3, matrix products, fold_step(): jnp.dot(queries, key_rows.T, preferred_element_type=jnp.float32)  2.48 us
  transfers between devices with their start and end apart: 9, of which 6 were waited for; matrix products, arithmetic and copies ran while one was open for 8% of the time, Pallas kernels for 0%

commit v1 on v0

v1 whole, which is shorter than its diff:
```python
import functools
import math

import jax
import jax.numpy as jnp
from jax import lax
from jax.experimental import pallas as pl
from jax.experimental.pallas import tpu as pltpu
from jax.sharding import PartitionSpec as P

MESH = pl.DeviceIdType.MESH
OFFSETS = 3
LENGTH_Z = 8
LENGTH_Y = 4
LENGTH_X = 4
PIECES = 4
SLOTS = 5
ROW_BLOCK = 256
score_factor = 2.5


def device_at(x, y, z, core):
    return ((x * 2 + y % 2) * LENGTH_Z + z, (y // 2) * 2 + core)


def kernel(
    features,
    select,
    validity,
    gain,
    out,
    keys,
    queries,
    votes_in,
    gains,
    own_flag,
    flags,
    high,
    total,
    weighted,
    chosen,
    numerator,
    local_sem,
    arrive,
    sent_up,
    sent_side,
    sent_core,
    flag_arrive,
    flag_sent,
):
    rows, channels = queries.shape
    ticks = OFFSETS * PIECES
    piece = rows // PIECES
    to_exponent = score_factor / math.sqrt(channels) * math.log2(math.e)

    section, tile = lax.axis_index("sec"), lax.axis_index("tile")
    z = section % LENGTH_Z
    x = section // (2 * LENGTH_Z)
    y = (tile // 2) * 2 + (section // LENGTH_Z) % 2
    core = tile % 2
    first = z == 0
    odd = y % 2
    last_z = z == LENGTH_Z - 1

    up = device_at(
        jnp.where(last_z, (x + odd) % LENGTH_X, x), y, (z + 1) % LENGTH_Z, core
    )
    down = device_at(
        jnp.where(first, (x + LENGTH_X - odd) % LENGTH_X, x), y, (z + LENGTH_Z - 1) % LENGTH_Z, core
    )
    partner = device_at(x, y, z, 1 - core)
    pair = device_at(x, (y + 2) % LENGTH_Y, z, core)
    right = device_at(x, (y + 1) % LENGTH_Y, z, core)
    left = device_at(x, (y + 3) % LENGTH_Y, z, core)

    copy_queries = pltpu.make_async_copy(features.at[0], queries, local_sem.at[0])
    copy_votes = pltpu.make_async_copy(select, votes_in, local_sem.at[1])
    copy_gains = pltpu.make_async_copy(gain, gains, local_sem.at[2])
    copy_flag = pltpu.make_async_copy(validity, own_flag, local_sem.at[3])
    copy_flag.start()
    copy_queries.start()
    copy_votes.start()
    copy_gains.start()

    barrier = pltpu.get_barrier_semaphore()

    def greet(target):
        pl.semaphore_signal(barrier, inc=1, device_id=target, device_id_type=MESH)

    greet(down)
    greet(partner)

    @pl.when(first)
    def _():
        greet(left)
        greet(right)
        pl.semaphore_wait(barrier, 4)

    @pl.when(jnp.logical_not(first))
    def _():
        greet(pair)
        pl.semaphore_wait(barrier, 3)

    def send(source, tick, slot, sem, target):
        return pltpu.make_async_remote_copy(
            src_ref=source,
            dst_ref=keys.at[tick, slot],
            send_sem=sem,
            recv_sem=arrive.at[tick, slot],
            device_id=target,
            device_id_type=MESH,
        )

    def own_piece(j):
        return features.at[0, pl.ds(j * piece, piece)]

    def send_flag(source, slot, sem, target):
        return pltpu.make_async_remote_copy(
            src_ref=source,
            dst_ref=flags.at[slot],
            send_sem=sem,
            recv_sem=flag_arrive.at[slot],
            device_id=target,
            device_id_type=MESH,
        )

    def send_own_flag():
        return send_flag(own_flag, 0, flag_sent.at[0], up)

    for j in range(PIECES):
        send(own_piece(j), j, 0, sent_up.at[j], up).start()
    copy_flag.wait()
    send_own_flag().start()
    copy_queries.wait()
    copy_votes.wait()
    copy_gains.wait()

    numerator[...] = jnp.zeros_like(numerator)

    def wait_for(tick, slot):
        pltpu.make_async_copy(keys.at[tick, slot], keys.at[tick, slot], arrive.at[tick, slot]).wait()

    def relay_up(i, slot):
        return send(keys.at[i, slot], i + PIECES, 0, sent_up.at[i + PIECES], up)

    def to_pair(i):
        return send(keys.at[i, 0], i, 1, sent_side.at[0, i], pair)

    def to_right(i):
        return send(keys.at[i, 0], i, 4, sent_side.at[0, i], right)

    def to_left(i):
        return send(keys.at[i, 0], i, 1, sent_side.at[1, i], left)

    def to_core(i, source, slot):
        return send(keys.at[i, source], i, slot, sent_core.at[slot - 2, i], partner)

    def take_from_below(i):
        wait_for(i, 0)

        @pl.when(first)
        def _():
            to_right(i).start()
            to_left(i).start()

        @pl.when(jnp.logical_not(first))
        def _():
            @pl.when(i < ticks - PIECES)
            def _():
                relay_up(i, 0).start()

            to_pair(i).start()
            to_core(i, 0, 2).start()

    def take_from_side(i):
        @pl.when(first)
        def _():
            wait_for(i, 4)

            @pl.when(i < ticks - PIECES)
            def _():
                relay_up(i, 4).start()

            to_core(i, 4, 2).start()

        wait_for(i, 1)
        to_core(i, 1, 3).start()

    start = jnp.where(first, 1, 0)

    def match(i):
        wait_for(i, 2)
        wait_for(i, 3)
        offset = i // PIECES

        @pl.when(i % PIECES == 0)
        def _():
            high[...] = jnp.full_like(high, -1e30)
            total[...] = jnp.zeros_like(total)
            weighted[...] = jnp.zeros_like(weighted)

        for block in range(rows // ROW_BLOCK):
            part = pl.ds(block * ROW_BLOCK, ROW_BLOCK)
            key_rows = keys[i, pl.ds(start, 4)].reshape(4 * piece, channels)
            scores = lax.dot_general(
                queries[part], key_rows, (((1,), (1,)), ((), ())), preferred_element_type=jnp.float32
            )
            before = high[part]
            now = jnp.maximum(before, jnp.max(scores, axis=1, keepdims=True) * to_exponent)
            weights = jnp.exp2(scores * to_exponent - now[:, :1])
            fade = jnp.exp2(before - now)
            partial = weights[:, :128]
            for lane in range(128, 4 * piece, 128):
                partial = partial + weights[:, lane : lane + 128]
            total[part] = fade * total[part] + partial
            weighted[part] = jnp.concatenate([fade, fade], axis=1) * weighted[part] + jnp.dot(
                weights.astype(jnp.bfloat16), key_rows, preferred_element_type=jnp.float32
            )
            high[part] = now

        @pl.when(i % PIECES == PIECES - 1)
        def _():
            vote = chosen[pl.ds(offset, 1)][0]
            factor = vote[:, :1] / jnp.sum(total[...], axis=1, keepdims=True)
            numerator[...] += factor * gains[pl.ds(offset, 1)] * weighted[...]

    picks = jnp.broadcast_to(votes_in[...], (128, rows)).T

    def flag_wait(slot):
        pltpu.make_async_copy(flags.at[slot], flags.at[slot], flag_arrive.at[slot]).wait()

    def relay_flag(offset):
        @pl.when(first)
        def _():
            flag_wait(offset)
            send_flag(flags.at[offset], 3 + offset, flag_sent.at[3 + offset], right).start()
            flag_wait(3 + offset)
            if offset < OFFSETS - 1:
                send_flag(flags.at[3 + offset], offset + 1, flag_sent.at[offset + 1], up).start()

        @pl.when(jnp.logical_not(first))
        def _():
            flag_wait(offset)
            if offset < OFFSETS - 1:
                send_flag(flags.at[offset], offset + 1, flag_sent.at[offset + 1], up).start()

    def vote_of(offset):
        usable = flags[jnp.where(first, 3 + offset, offset), 0]
        usable = jnp.where(section >= offset + 1, usable, 0).astype(jnp.float32)
        return (picks // 2**offset % 2).astype(jnp.float32) * usable

    def step(i, carry):
        @pl.when(i < ticks)
        def _():
            take_from_below(i)

        @pl.when(jnp.logical_and(i >= 2, i < ticks + 2))
        def _():
            take_from_side(i - 2)

        for offset in range(OFFSETS):
            @pl.when(i == offset * PIECES + 2)
            def _():
                relay_flag(offset)
                chosen[offset] = vote_of(offset)

        @pl.when(i >= 3)
        def _():
            match(i - 3)

        return carry

    lax.fori_loop(0, ticks + 3, step, 0)

    count = chosen[0] + chosen[1] + chosen[2]
    out[0] = (numerator[...] / jnp.maximum(count, 1.0)[:, :1]).astype(jnp.bfloat16)

    def finish(i, carry):
        @pl.when(i < PIECES)
        def _():
            send(own_piece(i), i, 0, sent_up.at[i], up).wait_send()

        @pl.when(first)
        def _():
            @pl.when(i < ticks - PIECES)
            def _():
                relay_up(i, 4).wait_send()

            to_right(i).wait_send()
            to_left(i).wait_send()
            to_core(i, 4, 2).wait_send()

        @pl.when(jnp.logical_not(first))
        def _():
            @pl.when(i < ticks - PIECES)
            def _():
                relay_up(i, 0).wait_send()

            to_pair(i).wait_send()
            to_core(i, 0, 2).wait_send()

        to_core(i, 1, 3).wait_send()
        return carry

    lax.fori_loop(0, ticks, finish, 0)
    send_own_flag().wait_send()
    for offset in range(OFFSETS):
        @pl.when(first)
        def _():
            send_flag(flags.at[offset], 3 + offset, flag_sent.at[3 + offset], right).wait_send()

        if offset < OFFSETS - 1:
            send_flag(flags.at[offset], offset + 1, flag_sent.at[offset + 1], up).wait_send()


def shards(features, select, validity, offset_gain):
    rows, channels = features.shape[1:]
    ticks = OFFSETS * PIECES
    anywhere = pl.BlockSpec(memory_space=pl.ANY)
    dma = pltpu.SemaphoreType.DMA
    return pl.pallas_call(
        kernel,
        out_shape=jax.ShapeDtypeStruct(features.shape, jnp.bfloat16),
        in_specs=[anywhere] * 4,
        out_specs=pl.BlockSpec(memory_space=pltpu.VMEM),
        scratch_shapes=[
            pltpu.VMEM((ticks, SLOTS, rows // PIECES, channels), jnp.bfloat16),
            pltpu.VMEM((rows, channels), jnp.bfloat16),
            pltpu.VMEM(select.shape, jnp.int32),
            pltpu.VMEM(offset_gain.shape, jnp.float32),
            pltpu.SMEM((1,), jnp.int32),
            pltpu.SMEM((2 * OFFSETS, 1), jnp.int32),
            pltpu.VMEM((rows, 128), jnp.float32),
            pltpu.VMEM((rows, 128), jnp.float32),
            pltpu.VMEM((rows, channels), jnp.float32),
            pltpu.VMEM((OFFSETS, rows, 128), jnp.float32),
            pltpu.VMEM((rows, channels), jnp.float32),
            dma((4,)),
            dma((ticks, SLOTS)),
            dma((ticks,)),
            dma((2, ticks)),
            dma((2, ticks)),
            dma((2 * OFFSETS,)),
            dma((2 * OFFSETS,)),
        ],
        compiler_params=pltpu.CompilerParams(collective_id=0, has_side_effects=True),
    )(features, select, validity, offset_gain)


def solution(mesh):
    in_specs = (P("sec", "tile", None), P("sec", "tile"), P("sec"), P())
    out_specs = P("sec", "tile", None)
    return jax.shard_map(shards, mesh=mesh, in_specs=in_specs, out_specs=out_specs, check_vma=False)
```

time: 100 us -> 54.1 us (0.54)
  the two profiles are of different devices: /device:TPU:7 before, /device:TPU:1 now
where the time goes in v1:
time: 54.1 us; the launch traced here: 54 us
  Pallas kernels  51.6 us (95%)
  local copies, waits for them, and re-layouts  1.67 us (3%)
  between operations  0.66 us (1%)
    pallas_call x1, Pallas kernels, shards(): pl.pallas_call(kernel, out_shape=jax.ShapeDtypeStruct(features.shape, jnp...  51.6 us
    unnamed x1, local copies, waits for them, and re-layouts  1.67 us

profile of v1, /device:TPU:1, one launch (start us, length us, event | category | flops | bytes accessed | tf_op | source)
XLA Modules:
  0.0 54.0 jit_solution(18252714031615950057)
XLA Ops:
  0.7 51.6 %shard_map.46 = bf16[1,512,256]{2,1,0:T(8,128)(2,1)} custom-call(bf16[1,512,256]{2,1,0:T(8,128)(2,1)} %features.1, s32[1,512]{1,0:T(1,128)} %select.1, s32[1]{0:T(128)S(6)} %copy.6.validity, f32[3,256]{1,0:T(4,128)} %gain.1), custom_call_target="tpu_custom_call" | custom-call | tf_op jit(solution)/shard_map/pallas_call | solution.py:321
  52.3 1.7 %copy.7 = bf16[1,512,256]{2,1,0:T(8,128)(2,1)} copy(bf16[1,512,256]{2,1,0:T(8,128)(2,1)} %shard_map.46) | data formatting | bytes 524288

commit v2 on v1

v2 whole, which is shorter than its diff:
```python
import functools
import math

import jax
import jax.numpy as jnp
from jax import lax
from jax.experimental import pallas as pl
from jax.experimental.pallas import tpu as pltpu
from jax.sharding import PartitionSpec as P

MESH = pl.DeviceIdType.MESH
OFFSETS = 3
LENGTH_Z = 8
LENGTH_Y = 4
LENGTH_X = 4
PIECES = 8
GROUP = 2
SIDE_LAG = 6
MATCH_LAG = 8
SLOTS = 5
ROW_BLOCK = 256
score_factor = 2.5


def device_at(x, y, z, core):
    return ((x * 2 + y % 2) * LENGTH_Z + z, (y // 2) * 2 + core)


def kernel(
    features,
    select,
    validity,
    gain,
    out,
    keys,
    queries,
    votes_in,
    gains,
    own_flag,
    flags,
    high,
    total,
    weighted,
    chosen,
    numerator,
    count,
    local_sem,
    arrive,
    sent,
    flag_arrive,
    flag_sent,
):
    rows, channels = queries.shape
    ticks = OFFSETS * PIECES
    groups = PIECES // GROUP
    sections = lax.axis_size("sec")
    piece = rows // PIECES
    to_exponent = score_factor / math.sqrt(channels) * math.log2(math.e)

    section, tile = lax.axis_index("sec"), lax.axis_index("tile")
    z = section % LENGTH_Z
    x = section // (2 * LENGTH_Z)
    y = (tile // 2) * 2 + (section // LENGTH_Z) % 2
    core = tile % 2
    first = z == 0
    odd = y % 2
    last_z = z == LENGTH_Z - 1

    up = device_at(
        jnp.where(last_z, (x + odd) % LENGTH_X, x), y, (z + 1) % LENGTH_Z, core
    )
    down = device_at(
        jnp.where(first, (x + LENGTH_X - odd) % LENGTH_X, x), y, (z + LENGTH_Z - 1) % LENGTH_Z, core
    )
    partner = device_at(x, y, z, 1 - core)
    pair = device_at(x, (y + 2) % LENGTH_Y, z, core)
    right = device_at(x, (y + 1) % LENGTH_Y, z, core)
    left = device_at(x, (y + 3) % LENGTH_Y, z, core)

    copy_queries = pltpu.make_async_copy(features.at[0], queries, local_sem.at[0])
    copy_votes = pltpu.make_async_copy(select, votes_in, local_sem.at[1])
    copy_gains = pltpu.make_async_copy(gain, gains, local_sem.at[2])
    copy_flag = pltpu.make_async_copy(validity, own_flag, local_sem.at[3])
    copy_flag.start()
    copy_queries.start()
    copy_votes.start()
    copy_gains.start()

    barrier = pltpu.get_barrier_semaphore()

    def greet(target):
        pl.semaphore_signal(barrier, inc=1, device_id=target, device_id_type=MESH)

    greet(down)
    greet(partner)
    for offset in range(OFFSETS):
        greet(((section + sections - offset - 1) % sections, tile))

    @pl.when(first)
    def _():
        greet(left)
        greet(right)

    @pl.when(jnp.logical_not(first))
    def _():
        greet(pair)

    copy_votes.wait()
    copy_gains.wait()
    picks = jnp.broadcast_to(votes_in[...], (128, rows)).T
    for offset in range(OFFSETS):
        chosen[offset] = (picks // 2**offset % 2).astype(jnp.float32)
    numerator[...] = jnp.zeros_like(numerator)
    count[...] = jnp.zeros_like(count)
    pl.semaphore_wait(barrier, 3 + OFFSETS + jnp.where(first, 1, 0))

    def send(source, tick, slot, sem, target):
        return pltpu.make_async_remote_copy(
            src_ref=source,
            dst_ref=keys.at[tick, slot],
            send_sem=sem,
            recv_sem=arrive.at[tick, slot],
            device_id=target,
            device_id_type=MESH,
        )

    def own_piece(j):
        return features.at[0, pl.ds(j * piece, piece)]

    def send_flag(offset):
        return pltpu.make_async_remote_copy(
            src_ref=own_flag,
            dst_ref=flags.at[offset],
            send_sem=flag_sent.at[offset],
            recv_sem=flag_arrive.at[offset],
            device_id=((section + offset + 1) % sections, tile),
            device_id_type=MESH,
        )

    copy_flag.wait()
    for offset in range(OFFSETS):
        send_flag(offset).start()
    for j in range(PIECES):
        send(own_piece(j), j, 0, sent, up).start()
    copy_queries.wait()

    def wait_for(tick, slot):
        pltpu.make_async_copy(keys.at[tick, slot], keys.at[tick, slot], arrive.at[tick, slot]).wait()

    def relay_up(i, slot):
        return send(keys.at[i, slot], i + PIECES, 0, sent, up)

    def to_pair(i):
        return send(keys.at[i, 0], i, 1, sent, pair)

    def to_right(i):
        return send(keys.at[i, 0], i, 4, sent, right)

    def to_left(i):
        return send(keys.at[i, 0], i, 1, sent, left)

    def to_core(i, source, slot):
        return send(keys.at[i, source], i, slot, sent, partner)

    def take_from_below(i):
        wait_for(i, 0)

        @pl.when(first)
        def _():
            to_right(i).start()
            to_left(i).start()

        @pl.when(jnp.logical_not(first))
        def _():
            @pl.when(i < ticks - PIECES)
            def _():
                relay_up(i, 0).start()

            to_pair(i).start()
            to_core(i, 0, 2).start()

    def take_from_side(i):
        @pl.when(first)
        def _():
            wait_for(i, 4)

            @pl.when(i < ticks - PIECES)
            def _():
                relay_up(i, 4).start()

            to_core(i, 4, 2).start()

        wait_for(i, 1)
        to_core(i, 1, 3).start()

    start = jnp.where(first, 1, 0)

    def match(g):
        for k in range(GROUP):
            wait_for(g * GROUP + k, 2)
            wait_for(g * GROUP + k, 3)
        offset = g // groups

        @pl.when(g % groups == 0)
        def _():
            high[...] = jnp.full_like(high, -1e30)
            total[...] = jnp.zeros_like(total)
            weighted[...] = jnp.zeros_like(weighted)

        for block in range(rows // ROW_BLOCK):
            part = pl.ds(block * ROW_BLOCK, ROW_BLOCK)
            key_rows = keys[pl.ds(g * GROUP, GROUP), pl.ds(start, 4)].reshape(GROUP * 4 * piece, channels)
            scores = lax.dot_general(
                queries[part], key_rows, (((1,), (1,)), ((), ())), preferred_element_type=jnp.float32
            )
            before = high[part]
            now = jnp.maximum(before, jnp.max(scores, axis=1, keepdims=True) * to_exponent)
            weights = jnp.exp2(scores * to_exponent - now[:, :1])
            fade = jnp.exp2(before - now)
            partial = weights[:, :128]
            for lane in range(128, GROUP * 4 * piece, 128):
                partial = partial + weights[:, lane : lane + 128]
            total[part] = fade * total[part] + partial
            weighted[part] = jnp.concatenate([fade, fade], axis=1) * weighted[part] + jnp.dot(
                weights.astype(jnp.bfloat16), key_rows, preferred_element_type=jnp.float32
            )
            high[part] = now

        @pl.when(g % groups == groups - 1)
        def _():
            pltpu.make_async_copy(flags.at[offset], flags.at[offset], flag_arrive.at[offset]).wait()
            usable = jnp.where(section > offset, flags[offset, 0], 0).astype(jnp.float32)
            vote = chosen[pl.ds(offset, 1)][0] * usable
            count[...] += vote
            factor = vote[:, :1] / jnp.sum(total[...], axis=1, keepdims=True)
            numerator[...] += factor * gains[pl.ds(offset, 1)] * weighted[...]

    def step(i, carry):
        @pl.when(i < ticks)
        def _():
            take_from_below(i)

        @pl.when(jnp.logical_and(i >= SIDE_LAG, i < ticks + SIDE_LAG))
        def _():
            take_from_side(i - SIDE_LAG)

        @pl.when(jnp.logical_and(i >= MATCH_LAG + GROUP - 1, (i - MATCH_LAG) % GROUP == GROUP - 1))
        def _():
            match((i - MATCH_LAG) // GROUP)

        return carry

    lax.fori_loop(0, ticks + MATCH_LAG, step, 0)

    out[0] = (numerator[...] / jnp.maximum(count[...], 1.0)[:, :1]).astype(jnp.bfloat16)

    def wait_sent(slots):
        everything = keys.at[:, pl.ds(0, slots)]
        pltpu.make_async_copy(everything, everything, sent).wait()

    @pl.when(first)
    def _():
        wait_sent(5)

    @pl.when(jnp.logical_not(first))
    def _():
        wait_sent(4)

    for offset in range(OFFSETS):
        send_flag(offset).wait_send()


def shards(features, select, validity, offset_gain):
    rows, channels = features.shape[1:]
    ticks = OFFSETS * PIECES
    anywhere = pl.BlockSpec(memory_space=pltpu.HBM)
    dma = pltpu.SemaphoreType.DMA
    return pl.pallas_call(
        kernel,
        out_shape=jax.ShapeDtypeStruct(features.shape, jnp.bfloat16),
        in_specs=[anywhere] * 4,
        out_specs=pl.BlockSpec(memory_space=pltpu.VMEM),
        scratch_shapes=[
            pltpu.VMEM((ticks, SLOTS, rows // PIECES, channels), jnp.bfloat16),
            pltpu.VMEM((rows, channels), jnp.bfloat16),
            pltpu.VMEM(select.shape, jnp.int32),
            pltpu.VMEM(offset_gain.shape, jnp.float32),
            pltpu.SMEM((1,), jnp.int32),
            pltpu.SMEM((OFFSETS, 1), jnp.int32),
            pltpu.VMEM((rows, 128), jnp.float32),
            pltpu.VMEM((rows, 128), jnp.float32),
            pltpu.VMEM((rows, channels), jnp.float32),
            pltpu.VMEM((OFFSETS, rows, 128), jnp.float32),
            pltpu.VMEM((rows, channels), jnp.float32),
            pltpu.VMEM((rows, 128), jnp.float32),
            dma((4,)),
            dma((ticks, SLOTS)),
            dma,
            dma((OFFSETS,)),
            dma((OFFSETS,)),
        ],
        compiler_params=pltpu.CompilerParams(collective_id=0, has_side_effects=True),
    )(features, select, validity, offset_gain)


def solution(mesh):
    in_specs = (P("sec", "tile", None), P("sec", "tile"), P("sec"), P())
    out_specs = P("sec", "tile", None)
    return jax.shard_map(shards, mesh=mesh, in_specs=in_specs, out_specs=out_specs, check_vma=False)
```

time: 54.1 us -> 41.5 us (0.77)
  Pallas kernels: 51.6 us -> 39.1 us
    pallas_call x1, Pallas kernels: 51.6 us -> 39.1 us  [shards(): pl.pallas_call(kernel, out_shape=jax.ShapeDtypeStruct(features.shape, jnp...]
where the time goes in v2:
time: 41.5 us; the launch traced here: 41.4 us
  Pallas kernels  39.1 us (94%)
  local copies, waits for them, and re-layouts  1.67 us (4%)
  between operations  0.66 us (2%)
    pallas_call x1, Pallas kernels, shards(): pl.pallas_call(kernel, out_shape=jax.ShapeDtypeStruct(features.shape, jnp...  39.1 us
    unnamed x1, local copies, waits for them, and re-layouts  1.67 us

profile of v2, /device:TPU:1, one launch (start us, length us, event | category | flops | bytes accessed | tf_op | source)
XLA Modules:
  0.0 41.4 jit_solution(6833512662938111408)
XLA Ops:
  0.7 39.1 %shard_map.46 = bf16[1,512,256]{2,1,0:T(8,128)(2,1)} custom-call(bf16[1,512,256]{2,1,0:T(8,128)(2,1)} %features.1, s32[1,512]{1,0:T(1,128)} %select.1, s32[1]{0:T(128)S(6)} %copy.6.validity, f32[3,256]{1,0:T(4,128)} %gain.1), custom_call_target="tpu_custom_call" | custom-call | tf_op jit(solution)/shard_map/pallas_call | solution.py:278
  39.7 1.7 %copy.7 = bf16[1,512,256]{2,1,0:T(8,128)(2,1)} copy(bf16[1,512,256]{2,1,0:T(8,128)(2,1)} %shard_map.46) | data formatting | bytes 524288

commit v3 on v2

--- a/solution.py
+++ b/solution.py
@@ -65,6 +65,16 @@
     first = z == 0
     odd = y % 2
     last_z = z == LENGTH_Z - 1
+    sends_up = section < sections - 1
+
+    def crosses(offset):
+        return offset >= z
+
+    def comes_up(offset):
+        return jnp.logical_not(jnp.logical_and(jnp.logical_and(x == 0, odd == 1), crosses(offset)))
+
+    def usable_offset(offset):
+        return section > offset
 
     up = device_at(
         jnp.where(last_z, (x + odd) % LENGTH_X, x), y, (z + 1) % LENGTH_Z, core
@@ -96,12 +106,12 @@
     for offset in range(OFFSETS):
         greet(((section + sections - offset - 1) % sections, tile))
 
-    @pl.when(first)
+    @pl.when(z < OFFSETS)
     def _():
         greet(left)
         greet(right)
 
-    @pl.when(jnp.logical_not(first))
+    @pl.when(z > 0)
     def _():
         greet(pair)
 
@@ -112,7 +122,7 @@
         chosen[offset] = (picks // 2**offset % 2).astype(jnp.float32)
     numerator[...] = jnp.zeros_like(numerator)
     count[...] = jnp.zeros_like(count)
-    pl.semaphore_wait(barrier, 3 + OFFSETS + jnp.where(first, 1, 0))
+    pl.semaphore_wait(barrier, 2 + OFFSETS + jnp.where(z < OFFSETS, 2, 0) + jnp.where(z > 0, 1, 0))
 
     def send(source, tick, slot, sem, target):
         return pltpu.make_async_remote_copy(
@@ -140,66 +150,60 @@
     copy_flag.wait()
     for offset in range(OFFSETS):
         send_flag(offset).start()
-    for j in range(PIECES):
-        send(own_piece(j), j, 0, sent, up).start()
+
+    @pl.when(sends_up)
+    def _():
+        for j in range(PIECES):
+            send(own_piece(j), j, 0, sent.at[0, 0], up).start()
+
     copy_queries.wait()
 
     def wait_for(tick, slot):
         pltpu.make_async_copy(keys.at[tick, slot], keys.at[tick, slot], arrive.at[tick, slot]).wait()
 
-    def relay_up(i, slot):
-        return send(keys.at[i, slot], i + PIECES, 0, sent, up)
-
-    def to_pair(i):
-        return send(keys.at[i, 0], i, 1, sent, pair)
-
-    def to_right(i):
-        return send(keys.at[i, 0], i, 4, sent, right)
-
-    def to_left(i):
-        return send(keys.at[i, 0], i, 1, sent, left)
-
-    def to_core(i, source, slot):
-        return send(keys.at[i, source], i, slot, sent, partner)
-
     def take_from_below(i):
-        wait_for(i, 0)
-
-        @pl.when(first)
-        def _():
-            to_right(i).start()
-            to_left(i).start()
-
-        @pl.when(jnp.logical_not(first))
-        def _():
-            @pl.when(i < ticks - PIECES)
-            def _():
-                relay_up(i, 0).start()
-
-            to_pair(i).start()
-            to_core(i, 0, 2).start()
+        offset = i // PIECES
+
+        @pl.when(comes_up(offset))
+        def _():
+            wait_for(i, 0)
+
+            @pl.when(jnp.logical_and(sends_up, offset < OFFSETS - 1))
+            def _():
+                send(keys.at[i, 0], i + PIECES, 0, sent.at[0, offset + 1], up).start()
+
+            @pl.when(crosses(offset))
+            def _():
+                send(keys.at[i, 0], i, 4, sent.at[1, offset], right).start()
+                send(keys.at[i, 0], i, 1, sent.at[2, offset], left).start()
+
+            @pl.when(jnp.logical_not(crosses(offset)))
+            def _():
+                send(keys.at[i, 0], i, 1, sent.at[1, offset], pair).start()
+                send(keys.at[i, 0], i, 2, sent.at[3, offset], partner).start()
 
     def take_from_side(i):
-        @pl.when(first)
-        def _():
-            wait_for(i, 4)
-
-            @pl.when(i < ticks - PIECES)
-            def _():
-                relay_up(i, 4).start()
-
-            to_core(i, 4, 2).start()
-
-        wait_for(i, 1)
-        to_core(i, 1, 3).start()
-
-    start = jnp.where(first, 1, 0)
+        offset = i // PIECES
+
+        @pl.when(usable_offset(offset))
+        def _():
+            @pl.when(crosses(offset))
+            def _():
+                wait_for(i, 4)
+                send(keys.at[i, 4], i, 2, sent.at[3, offset], partner).start()
+
+            wait_for(i, 1)
+            send(keys.at[i, 1], i, 3, sent.at[4, offset], partner).start()
+
+    def flag_wait(offset):
+        pltpu.make_async_copy(flags.at[offset], flags.at[offset], flag_arrive.at[offset]).wait()
 
     def match(g):
         for k in range(GROUP):
             wait_for(g * GROUP + k, 2)
             wait_for(g * GROUP + k, 3)
         offset = g // groups
+        start = jnp.where(crosses(offset), 1, 0)
 
         @pl.when(g % groups == 0)
         def _():
@@ -228,8 +232,8 @@
 
         @pl.when(g % groups == groups - 1)
         def _():
-            pltpu.make_async_copy(flags.at[offset], flags.at[offset], flag_arrive.at[offset]).wait()
-            usable = jnp.where(section > offset, flags[offset, 0], 0).astype(jnp.float32)
+            flag_wait(offset)
+            usable = flags[offset, 0].astype(jnp.float32)
             vote = chosen[pl.ds(offset, 1)][0] * usable
             count[...] += vote
             factor = vote[:, :1] / jnp.sum(total[...], axis=1, keepdims=True)
@@ -246,7 +250,11 @@
 
         @pl.when(jnp.logical_and(i >= MATCH_LAG + GROUP - 1, (i - MATCH_LAG) % GROUP == GROUP - 1))
         def _():
-            match((i - MATCH_LAG) // GROUP)
+            g = (i - MATCH_LAG) // GROUP
+
+            @pl.when(usable_offset(g // groups))
+            def _():
+                match(g)
 
         return carry
 
@@ -254,19 +262,26 @@
 
     out[0] = (numerator[...] / jnp.maximum(count[...], 1.0)[:, :1]).astype(jnp.bfloat16)
 
-    def wait_sent(slots):
-        everything = keys.at[:, pl.ds(0, slots)]
-        pltpu.make_async_copy(everything, everything, sent).wait()
-
-    @pl.when(first)
-    def _():
-        wait_sent(5)
-
-    @pl.when(jnp.logical_not(first))
-    def _():
-        wait_sent(4)
-
-    for offset in range(OFFSETS):
+    def wait_sent(kind, offset, sends):
+        @pl.when(sends)
+        def _():
+            tile_sent = keys.at[pl.ds(0, PIECES), 0]
+            pltpu.make_async_copy(tile_sent, tile_sent, sent.at[kind, offset]).wait()
+
+    wait_sent(0, 0, sends_up)
+    for offset in range(OFFSETS):
+        if offset > 0:
+            wait_sent(0, offset, jnp.logical_and(sends_up, comes_up(offset - 1)))
+        wait_sent(1, offset, comes_up(offset))
+        wait_sent(2, offset, jnp.logical_and(comes_up(offset), crosses(offset)))
+        wait_sent(3, offset, usable_offset(offset))
+        wait_sent(4, offset, usable_offset(offset))
+
+    for offset in range(OFFSETS):
+        @pl.when(jnp.logical_not(usable_offset(offset)))
+        def _():
+            flag_wait(offset)
+
         send_flag(offset).wait_send()
 
 
@@ -295,7 +310,7 @@
             pltpu.VMEM((rows, 128), jnp.float32),
             dma((4,)),
             dma((ticks, SLOTS)),
-            dma,
+            dma((5, OFFSETS)),
             dma((OFFSETS,)),
             dma((OFFSETS,)),
         ],

time: 41.5 us -> 38.9 us (0.937)
  the two profiles are of different devices: /device:TPU:1 before, /device:TPU:7 now
where the time goes in v3:
time: 38.9 us; the launch traced here: 38.8 us
  Pallas kernels  36.5 us (94%)
  local copies, waits for them, and re-layouts  1.67 us (4%)
  between operations  0.66 us (2%)
    pallas_call x1, Pallas kernels, shards(): pl.pallas_call(kernel, out_shape=jax.ShapeDtypeStruct(features.shape, jnp...  36.5 us
    unnamed x1, local copies, waits for them, and re-layouts  1.67 us

profile of v3, /device:TPU:7, one launch (start us, length us, event | category | flops | bytes accessed | tf_op | source)
XLA Modules:
  0.0 38.8 jit_solution(1917907778032398821)
XLA Ops:
  0.7 36.5 %shard_map.46 = bf16[1,512,256]{2,1,0:T(8,128)(2,1)} custom-call(bf16[1,512,256]{2,1,0:T(8,128)(2,1)} %features.1, s32[1,512]{1,0:T(1,128)} %select.1, s32[1]{0:T(128)S(6)} %copy.6.validity, f32[3,256]{1,0:T(4,128)} %gain.1), custom_call_target="tpu_custom_call" | custom-call | tf_op jit(solution)/shard_map/pallas_call | solution.py:293
  37.1 1.7 %copy.7 = bf16[1,512,256]{2,1,0:T(8,128)(2,1)} copy(bf16[1,512,256]{2,1,0:T(8,128)(2,1)} %shard_map.46) | data formatting | bytes 524288

commit v4 on v3

--- a/solution.py
+++ b/solution.py
@@ -24,6 +24,13 @@
 
 def device_at(x, y, z, core):
     return ((x * 2 + y % 2) * LENGTH_Z + z, (y // 2) * 2 + core)
+
+
+def lane_sum(weights):
+    lanes = [weights[:, lane : lane + 128] for lane in range(0, weights.shape[1], 128)]
+    while len(lanes) > 1:
+        lanes = [a + b for a, b in zip(lanes[::2], lanes[1::2])]
+    return lanes[0]
 
 
 def kernel(
@@ -211,24 +218,28 @@
             total[...] = jnp.zeros_like(total)
             weighted[...] = jnp.zeros_like(weighted)
 
-        for block in range(rows // ROW_BLOCK):
-            part = pl.ds(block * ROW_BLOCK, ROW_BLOCK)
-            key_rows = keys[pl.ds(g * GROUP, GROUP), pl.ds(start, 4)].reshape(GROUP * 4 * piece, channels)
-            scores = lax.dot_general(
+        key_rows = keys[pl.ds(g * GROUP, GROUP), pl.ds(start, 4)].reshape(GROUP * 4 * piece, channels)
+        parts = [pl.ds(block * ROW_BLOCK, ROW_BLOCK) for block in range(rows // ROW_BLOCK)]
+        scores = [
+            lax.dot_general(
                 queries[part], key_rows, (((1,), (1,)), ((), ())), preferred_element_type=jnp.float32
             )
+            for part in parts
+        ]
+        rounded, fades = [], []
+        for part, block in zip(parts, scores):
             before = high[part]
-            now = jnp.maximum(before, jnp.max(scores, axis=1, keepdims=True) * to_exponent)
-            weights = jnp.exp2(scores * to_exponent - now[:, :1])
+            now = jnp.maximum(before, jnp.max(block, axis=1, keepdims=True) * to_exponent)
+            weights = jnp.exp2(block * to_exponent - now[:, :1])
             fade = jnp.exp2(before - now)
-            partial = weights[:, :128]
-            for lane in range(128, GROUP * 4 * piece, 128):
-                partial = partial + weights[:, lane : lane + 128]
-            total[part] = fade * total[part] + partial
-            weighted[part] = jnp.concatenate([fade, fade], axis=1) * weighted[part] + jnp.dot(
-                weights.astype(jnp.bfloat16), key_rows, preferred_element_type=jnp.float32
+            total[part] = fade * total[part] + lane_sum(weights)
+            high[part] = now
+            rounded.append(weights.astype(jnp.bfloat16))
+            fades.append(jnp.concatenate([fade, fade], axis=1))
+        for part, weights, fade in zip(parts, rounded, fades):
+            weighted[part] = fade * weighted[part] + jnp.dot(
+                weights, key_rows, preferred_element_type=jnp.float32
             )
-            high[part] = now
 
         @pl.when(g % groups == groups - 1)
         def _():
@@ -283,6 +294,10 @@
             flag_wait(offset)
 
         send_flag(offset).wait_send()
+
+
+def in_hbm(array):
+    return pltpu.with_memory_space_constraint(array, pltpu.HBM)
 
 
 def shards(features, select, validity, offset_gain):
@@ -314,8 +329,8 @@
             dma((OFFSETS,)),
             dma((OFFSETS,)),
         ],
-        compiler_params=pltpu.CompilerParams(collective_id=0, has_side_effects=True),
-    )(features, select, validity, offset_gain)
+        compiler_params=pltpu.CompilerParams(collective_id=0, has_side_effects=True, vmem_limit_bytes=20 << 20),
+    )(in_hbm(features), in_hbm(select), validity, in_hbm(offset_gain))
 
 
 def solution(mesh):

time: 38.9 us -> 36.8 us (0.946)
  Pallas kernels: 36.5 us -> 35.3 us
  local copies, waits for them, and re-layouts: 1.67 us -> 0.71 us
    pallas_call x1, Pallas kernels: 36.5 us -> 35.3 us  [shards(): pl.pallas_call(kernel, out_shape=jax.ShapeDtypeStruct(features.shape, jnp...]
    unnamed x1, local copies, waits for them, and re-layouts: 1.67 us -> 0.71 us
where the time goes in v4:
time: 36.8 us; the launch traced here: 36.7 us
  Pallas kernels  35.3 us (96%)
  local copies, waits for them, and re-layouts  0.71 us (2%)
  between operations  0.66 us (2%)
    pallas_call x1, Pallas kernels, shards(): pl.pallas_call(kernel, out_shape=jax.ShapeDtypeStruct(features.shape, jnp...  35.3 us

profile of v4, /device:TPU:7, one launch (start us, length us, event | category | flops | bytes accessed | tf_op | source)
XLA Modules:
  0.0 36.7 jit_solution(14700224118905399003)
XLA Ops:
  0.7 35.3 %shard_map.46 = bf16[1,512,256]{2,1,0:T(8,128)(2,1)S(1)} custom-call(bf16[1,512,256]{2,1,0:T(8,128)(2,1)} %features.1, s32[1,512]{1,0:T(1,128)} %select.1, s32[1]{0:T(128)S(6)} %copy.6.validity, f32[3,256]{1,0:T(4,128)} %gain.1), custom_call_target="tpu_custom_call" | custom-call | tf_op jit(solution)/shard_map/pallas_call | solution.py:308
  36.0 0.7 %copy.7 = bf16[1,512,256]{2,1,0:T(8,128)(2,1)} copy(bf16[1,512,256]{2,1,0:T(8,128)(2,1)S(1)} %shard_map.46) | data formatting | bytes 524288

commit v5 on v4

--- a/solution.py
+++ b/solution.py
@@ -13,10 +13,10 @@
 LENGTH_Z = 8
 LENGTH_Y = 4
 LENGTH_X = 4
-PIECES = 8
-GROUP = 2
-SIDE_LAG = 6
-MATCH_LAG = 8
+PIECES = 4
+GROUP = 1
+SIDE_LAG = 4
+MATCH_LAG = 5
 SLOTS = 5
 ROW_BLOCK = 256
 score_factor = 2.5
@@ -155,14 +155,14 @@
         )
 
     copy_flag.wait()
-    for offset in range(OFFSETS):
-        send_flag(offset).start()
 
     @pl.when(sends_up)
     def _():
         for j in range(PIECES):
             send(own_piece(j), j, 0, sent.at[0, 0], up).start()
 
+    for offset in range(OFFSETS):
+        send_flag(offset).start()
     copy_queries.wait()
 
     def wait_for(tick, slot):
@@ -175,10 +175,6 @@
         def _():
             wait_for(i, 0)
 
-            @pl.when(jnp.logical_and(sends_up, offset < OFFSETS - 1))
-            def _():
-                send(keys.at[i, 0], i + PIECES, 0, sent.at[0, offset + 1], up).start()
-
             @pl.when(crosses(offset))
             def _():
                 send(keys.at[i, 0], i, 4, sent.at[1, offset], right).start()
@@ -188,6 +184,10 @@
             def _():
                 send(keys.at[i, 0], i, 1, sent.at[1, offset], pair).start()
                 send(keys.at[i, 0], i, 2, sent.at[3, offset], partner).start()
+
+            @pl.when(jnp.logical_and(sends_up, offset < OFFSETS - 1))
+            def _():
+                send(keys.at[i, 0], i + PIECES, 0, sent.at[0, offset + 1], up).start()
 
     def take_from_side(i):
         offset = i // PIECES
@@ -248,7 +248,15 @@
             vote = chosen[pl.ds(offset, 1)][0] * usable
             count[...] += vote
             factor = vote[:, :1] / jnp.sum(total[...], axis=1, keepdims=True)
-            numerator[...] += factor * gains[pl.ds(offset, 1)] * weighted[...]
+            result = numerator[...] + factor * gains[pl.ds(offset, 1)] * weighted[...]
+
+            @pl.when(offset < OFFSETS - 1)
+            def _():
+                numerator[...] = result
+
+            @pl.when(offset == OFFSETS - 1)
+            def _():
+                out[0] = (result / jnp.maximum(count[...], 1.0)[:, :1]).astype(jnp.bfloat16)
 
     def step(i, carry):
         @pl.when(i < ticks)
@@ -271,7 +279,9 @@
 
     lax.fori_loop(0, ticks + MATCH_LAG, step, 0)
 
-    out[0] = (numerator[...] / jnp.maximum(count[...], 1.0)[:, :1]).astype(jnp.bfloat16)
+    @pl.when(jnp.logical_not(usable_offset(OFFSETS - 1)))
+    def _():
+        out[0] = (numerator[...] / jnp.maximum(count[...], 1.0)[:, :1]).astype(jnp.bfloat16)
 
     def wait_sent(kind, offset, sends):
         @pl.when(sends)

time: 36.8 us -> 36.7 us (level)
  no operation moved by 1% of the time
where the time goes in v5:
time: 36.7 us; the launch traced here: 36.6 us
  Pallas kernels  35.2 us (96%)
  local copies, waits for them, and re-layouts  0.71 us (2%)
  between operations  0.66 us (2%)
    pallas_call x1, Pallas kernels, shards(): pl.pallas_call(kernel, out_shape=jax.ShapeDtypeStruct(features.shape, jnp...  35.2 us

profile of v5, /device:TPU:7, one launch (start us, length us, event | category | flops | bytes accessed | tf_op | source)
XLA Modules:
  0.0 36.6 jit_solution(7589224763554821464)
XLA Ops:
  0.7 35.2 %shard_map.46 = bf16[1,512,256]{2,1,0:T(8,128)(2,1)S(1)} custom-call(bf16[1,512,256]{2,1,0:T(8,128)(2,1)} %features.1, s32[1,512]{1,0:T(1,128)} %select.1, s32[1]{0:T(128)S(6)} %copy.6.validity, f32[3,256]{1,0:T(4,128)} %gain.1), custom_call_target="tpu_custom_call" | custom-call | tf_op jit(solution)/shard_map/pallas_call | solution.py:318
  35.9 0.7 %copy.7 = bf16[1,512,256]{2,1,0:T(8,128)(2,1)} copy(bf16[1,512,256]{2,1,0:T(8,128)(2,1)S(1)} %shard_map.46) | data formatting | bytes 524288

commit v6 on v5

--- a/solution.py
+++ b/solution.py
@@ -229,9 +229,9 @@
         rounded, fades = [], []
         for part, block in zip(parts, scores):
             before = high[part]
-            now = jnp.maximum(before, jnp.max(block, axis=1, keepdims=True) * to_exponent)
-            weights = jnp.exp2(block * to_exponent - now[:, :1])
-            fade = jnp.exp2(before - now)
+            now = jnp.maximum(before, jnp.max(block, axis=1, keepdims=True))
+            weights = jnp.exp2((block - now[:, :1]) * to_exponent)
+            fade = jnp.exp2((before - now) * to_exponent)
             total[part] = fade * total[part] + lane_sum(weights)
             high[part] = now
             rounded.append(weights.astype(jnp.bfloat16))

time: 36.7 us -> 36.7 us (level)
  no operation moved by 1% of the time
where the time goes in v6:
time: 36.7 us; the launch traced here: 36.6 us
  Pallas kernels  35.2 us (96%)
  local copies, waits for them, and re-layouts  0.71 us (2%)
  between operations  0.66 us (2%)
    pallas_call x1, Pallas kernels, shards(): pl.pallas_call(kernel, out_shape=jax.ShapeDtypeStruct(features.shape, jnp...  35.2 us

profile of v6, /device:TPU:7, one launch (start us, length us, event | category | flops | bytes accessed | tf_op | source)
XLA Modules:
  0.0 36.6 jit_solution(7498257287862013380)
XLA Ops:
  0.7 35.2 %shard_map.46 = bf16[1,512,256]{2,1,0:T(8,128)(2,1)S(1)} custom-call(bf16[1,512,256]{2,1,0:T(8,128)(2,1)} %features.1, s32[1,512]{1,0:T(1,128)} %select.1, s32[1]{0:T(128)S(6)} %copy.6.validity, f32[3,256]{1,0:T(4,128)} %gain.1), custom_call_target="tpu_custom_call" | custom-call | tf_op jit(solution)/shard_map/pallas_call | solution.py:318
  35.9 0.7 %copy.7 = bf16[1,512,256]{2,1,0:T(8,128)(2,1)} copy(bf16[1,512,256]{2,1,0:T(8,128)(2,1)S(1)} %shard_map.46) | data formatting | bytes 524288
